TPU v7x, 32 devices: a whole 2x2x4 slice. The times are simulated.
32 devices in a mesh: groups: 2 (over x), tensor: 4 (over y, core), section: 4 (over z).
Axes of the slice: x: 2, y: 2, z: 4, core: 2. Of those that a mesh axis runs over, the one named last changes fastest.
Arguments:
- prompt: bfloat16 [128, 8192], P(('groups', 'section'), 'tensor'), parts along dimension 0, may hold values from -6 to 6
- norm_gain: float32 [8, 8192], P(('groups', 'section')), parts along dimension 0, may hold values from 0.5 to 1.5
- kept_ranks: int32 [8, 3], P(('groups', 'section')), parts along dimension 0, may hold values from 128 to 512, as said below
- gate_left: bfloat16 [8, 512, 8192], P('groups', 'tensor', 'section'), parts along dimension 0, may hold values from -0.0625 to 0.0625
- up_left: bfloat16 [8, 512, 8192], P('groups', 'tensor', 'section'), parts along dimension 0, may hold values from -0.0625 to 0.0625
- gate_right: bfloat16 [8, 512, 14336], P('groups', 'tensor', 'section'), parts along dimension 0, may hold values from -0.375 to 0.375
- up_right: bfloat16 [8, 512, 14336], P('groups', 'tensor', 'section'), parts along dimension 0, may hold values from -0.375 to 0.375
- down_left: bfloat16 [8, 512, 14336], P('groups', 'tensor', 'section'), parts along dimension 0, may hold values from -0.046875 to 0.046875
- down_right: bfloat16 [8, 8192, 512], P('groups', 'tensor', 'section'), parts along dimension 0, may hold values from -0.5 to 0.5
Outputs:
- final_stream: bfloat16 [128, 8192], P(('groups', 'section'), 'tensor'), parts along dimension 0
There are 2 independent parts, one for each index of `groups`. A program takes and returns all parts, laid end to end along the dimension named above; each array names one. Nothing has to cross between parts.
Inputs may be any that keep to these rules, and one draw needn't show every extreme that they name: `kept_ranks`: column 0, 1, 2 holds the rank kept for the gate, up and down matrices; the value 512 occurs in every draw.
All inputs are finite; a program needn't handle non-finite values.
Results may differ from a plain program's by a relative error of at most 0.035.
Values may be sent and summed in bfloat16 or wider, within the bound.
No kernel may reach another device: no remote copies, remote signals or barrier semaphores. Data moves between devices by JAX's collectives and lax.ppermute only.
A program may use at most 128 MiB of HBM per device.

v0:
```python
import jax
import jax.numpy as jnp
from jax import lax
from jax.sharding import PartitionSpec as P

RMAX = 512


def from_behind(block, axis, distance):
    devices = range(lax.axis_size(axis))
    route = [(i - distance, i) for i in devices if i - distance in devices]
    return lax.ppermute(block, axis, route)


def broadcast(array, axis, root):
    mine = lax.axis_index(axis) == root
    return lax.psum(jnp.where(mine, array, jnp.zeros_like(array)), axis)


def contract_last(left_side, right_side):
    return lax.dot_general(
        left_side, right_side, (((1,), (1,)), ((), ())), preferred_element_type=jnp.float32
    )


def body(
    prompt, norm_gain, kept_ranks, gate_left, up_left, gate_right, up_right, down_left, down_right
):
    section_count = lax.axis_size("section")
    tensor_rank = lax.axis_index("tensor")
    section_rank = lax.axis_index("section")
    gate_rows, up_rows, down_cols = (
        lax.all_to_all(gate_left, "section", split_axis=0, concat_axis=2, tiled=True),
        lax.all_to_all(up_left, "section", split_axis=0, concat_axis=2, tiled=True),
        lax.all_to_all(down_right, "section", split_axis=0, concat_axis=2, tiled=True),
    )
    gate_cols, up_cols, down_rows = (
        lax.all_to_all(
            lax.all_to_all(gate_right, "tensor", split_axis=2, concat_axis=1, tiled=True),
            "section",
            split_axis=0,
            concat_axis=2,
            tiled=True,
        ),
        lax.all_to_all(
            lax.all_to_all(up_right, "tensor", split_axis=2, concat_axis=1, tiled=True),
            "section",
            split_axis=0,
            concat_axis=2,
            tiled=True,
        ),
        lax.all_to_all(
            lax.all_to_all(down_left, "tensor", split_axis=2, concat_axis=1, tiled=True),
            "section",
            split_axis=0,
            concat_axis=2,
            tiled=True,
        ),
    )
    gate_rows, up_rows, down_cols = (gate_rows[0], up_rows[0], down_cols[0])
    gate_cols, up_cols, down_rows = (gate_cols[0], up_cols[0], down_rows[0])
    rank_block = gate_rows.shape[0]
    column_block = down_cols.shape[0]
    micro_rows = prompt.shape[0]
    positions = tensor_rank * rank_block + jnp.arange(rank_block, dtype=jnp.int32)
    gate_mask = (positions < kept_ranks[0, 0]).astype(jnp.float32)
    up_mask = (positions < kept_ranks[0, 1]).astype(jnp.float32)
    down_mask = (jnp.arange(RMAX, dtype=jnp.int32) < kept_ranks[0, 2]).astype(jnp.float32)
    norm_scale = norm_gain[0]
    own_start = tensor_rank * column_block
    prompt_rows = lax.all_gather(prompt, "section", axis=0, tiled=True)

    def layer_step(stream):
        float_stream = stream.astype(jnp.float32)
        variance = jnp.mean(float_stream * float_stream, axis=-1, keepdims=True)
        normed = (float_stream * lax.rsqrt(variance + 1e-05) * norm_scale).astype(jnp.bfloat16)
        gate_part = (contract_last(normed, gate_rows) * gate_mask).astype(jnp.bfloat16)
        up_part = (contract_last(normed, up_rows) * up_mask).astype(jnp.bfloat16)
        gate_low, up_low = (
            lax.all_gather(gate_part, "tensor", axis=1, tiled=True),
            lax.all_gather(up_part, "tensor", axis=1, tiled=True),
        )
        gate_values = jnp.dot(gate_low, gate_cols, preferred_element_type=jnp.float32)
        up_values = jnp.dot(up_low, up_cols, preferred_element_type=jnp.float32)
        hidden = (jax.nn.silu(gate_values) * up_values).astype(jnp.bfloat16)
        summed = lax.psum(contract_last(hidden, down_rows), "tensor")
        down_low = (summed * down_mask).astype(jnp.bfloat16)
        branch = contract_last(down_low, down_cols)
        own_columns = lax.dynamic_slice_in_dim(float_stream, own_start, column_block, 1)
        return (own_columns + branch).astype(jnp.bfloat16)

    incoming = jnp.zeros((micro_rows, column_block), jnp.bfloat16)
    results = jnp.zeros((micro_rows * section_count, column_block), jnp.bfloat16)

    def tick_body(tick_index, carry):
        incoming, results = carry
        entering = lax.dynamic_slice_in_dim(
            prompt_rows, jnp.minimum(tick_index, section_count - 1) * micro_rows, micro_rows, 0
        )
        current = jnp.where((section_rank == 0) & (tick_index < section_count), entering, incoming)
        stream = lax.all_gather(current, "tensor", axis=1, tiled=True)
        new_part = layer_step(stream)
        incoming = from_behind(new_part, "section", 1)
        finished = tick_index - (section_count - 1)
        slot_start = jnp.maximum(finished, 0) * micro_rows
        updated = lax.dynamic_update_slice_in_dim(results, new_part, slot_start, 0)
        results = jnp.where((section_rank == section_count - 1) & (finished >= 0), updated, results)
        return (incoming, results)

    incoming, results = lax.fori_loop(0, 2 * section_count - 1, tick_body, (incoming, results))
    delivered = broadcast(results, "section", section_count - 1)
    return lax.dynamic_slice_in_dim(delivered, section_rank * micro_rows, micro_rows, 0)


def solution(mesh):
    in_specs = (
        P(("groups", "section"), "tensor"),
        P(("groups", "section"), None),
        P(("groups", "section"), None),
        P("groups", "tensor", "section"),
        P("groups", "tensor", "section"),
        P("groups", "tensor", "section"),
        P("groups", "tensor", "section"),
        P("groups", "tensor", "section"),
        P("groups", "tensor", "section"),
    )
    out_specs = P(("groups", "section"), "tensor")
    return jax.shard_map(body, mesh=mesh, in_specs=in_specs, out_specs=out_specs, check_vma=False)
```

profile of v0, /device:TPU:0, one launch (start us, length us, event | category | flops | bytes accessed | tf_op | source)
XLA Modules:
  0.0 1003.2 jit_solution(816205238414276463)
XLA Ops:
  6.5 6.8 copy.26
  18.2 6.9 copy.30
  25.0 36.4 %all-to-all-done.1 = bf16[4,128,3584]{1,0,2:T(4,128)(2,1)} async-done(((bf16[4,128,3584]{1,0,2:T(4,128)(2,1)}), bf16[4,128,3584]{1,0,2:T(4,128)(2,1)}, u32[]{:S(2)}, u32[]{:S(2)}) %all-to-all-start.1) | async-done | bytes 3670048 | tf_op jit(solution)/shard_map/all_to_all | solution.py:39
  66.2 6.9 copy.33
  73.0 35.7 %all-to-all-done.4 = bf16[4,128,3584]{1,0,2:T(4,128)(2,1)} async-done(((bf16[4,128,3584]{1,0,2:T(4,128)(2,1)}), bf16[4,128,3584]{1,0,2:T(4,128)(2,1)}, u32[]{:S(2)}, u32[]{:S(2)}) %all-to-all-start.4) | async-done | bytes 3670048 | tf_op jit(solution)/shard_map/all_to_all | solution.py:46
  108.7 48.1 %all_to_all.144 = bf16[4,128,3584]{1,0,2:T(4,128)(2,1)} all-to-all(bf16[4,128,3584]{1,0,2:T(4,128)(2,1)} %copy.33), channel_id=1, replica_groups=mesh['groups'=2,'tensor'=4,'section'=4] {'tensor'}, dimensions={2} | all-to-all | bytes 7340032 | tf_op jit(solution)/shard_map/all_to_all | solution.py:53
  156.8 53.6 %all_to_all.145 = bf16[4,128,2048]{2,1,0:T(8,128)(2,1)} all-to-all(bf16[4,128,2048]{2,1,0:T(8,128)(2,1)S(1)} %copy-done.6), channel_id=1, replica_groups=mesh['groups'=2,'tensor'=4,'section'=4] {'section'}, dimensions={0} | all-to-all | bytes 4194304 | tf_op jit(solution)/shard_map/all_to_all | solution.py:33
  210.4 50.4 %all_to_all.146 = bf16[4,128,2048]{2,1,0:T(8,128)(2,1)} all-to-all(bf16[4,128,2048]{2,1,0:T(8,128)(2,1)S(1)} %copy-done.7), channel_id=1, replica_groups=mesh['groups'=2,'tensor'=4,'section'=4] {'section'}, dimensions={0} | all-to-all | bytes 4194304 | tf_op jit(solution)/shard_map/all_to_all | solution.py:34
  264.5 6.9 copy.27
  271.3 40.4 %all-to-all-done.8 = bf16[4,2048,128]{2,1,0:T(8,128)(2,1)S(1)} async-done(((bf16[4,2048,128]{2,1,0:T(8,128)(2,1)}), bf16[4,2048,128]{2,1,0:T(8,128)(2,1)S(1)}, u32[]{:S(2)}, u32[]{:S(2)}) %all-to-all-start.8) | async-done | bytes 2097184 | tf_op jit(solution)/shard_map/all_to_all | solution.py:35
  317.8 6.9 copy.31
  324.7 74.6 %all-to-all-done.2 = bf16[4,512,896]{2,1,0:T(8,128)(2,1)} async-done(((bf16[4,512,896]{2,1,0:T(8,128)(2,1)}), bf16[4,512,896]{2,1,0:T(8,128)(2,1)}, u32[]{:S(2)}, u32[]{:S(2)}) %all-to-all-start.2) | async-done | bytes 3670048 | tf_op jit(solution)/shard_map/all_to_all | solution.py:38
  404.1 7.0 copy.34
  411.0 74.6 %all-to-all-done.5 = bf16[4,512,896]{2,1,0:T(8,128)(2,1)} async-done(((bf16[4,512,896]{2,1,0:T(8,128)(2,1)}), bf16[4,512,896]{2,1,0:T(8,128)(2,1)}, u32[]{:S(2)}, u32[]{:S(2)}) %all-to-all-start.5) | async-done | bytes 3670048 | tf_op jit(solution)/shard_map/all_to_all | solution.py:45
  490.6 89.0 %all_gather.33 = bf16[64,2048]{1,0:T(8,128)(2,1)S(1)} all-gather(bf16[16,2048]{1,0:T(8,128)(2,1)S(1)} %copy-done.8), channel_id=1, replica_groups=mesh['groups'=2,'tensor'=4,'section'=4] {'section'}, dimensions={0}, use_global_device_ids=true | all-gather | bytes 327680 | tf_op jit(solution)/shard_map/all_gather | solution.py:71
  587.6 9.7 copy.36
  599.1 6.0 copy.28
  605.0 5.9 copy.37
  611.0 6.0 copy.32
  616.9 6.0 copy.38
  622.9 6.0 copy.35
  628.9 6.0 copy.39
  634.9 322.3 %while.19 = (s32[]{:T(128)}, bf16[16,2048]{1,0:T(8,128)(2,1)S(1)}, bf16[64,2048]{1,0:T(8,128)(2,1)S(1)}, pred[]{:T(512)}, bf16[64,2048]{1,0:T(8,128)(2,1)S(1)}, ...) while((s32[]{:T(128)}, bf16[16,2048]{1,0:T(8,128)(2,1)S(1)}, ...), condition=%wide.region_3.4_spmd.clone.clone, body=%wide.region_0.3_spmd.clone.clone.sunk | while | flops 278906656 | bytes 35412760 | solution.py:110
  635.0 5.8 all_gather.43
  661.0 11.4 %psum.25 = f32[16,512]{1,0:T(8,128)S(1)} all-reduce(f32[16,512]{1,0:T(8,128)S(1)} %fusion.54), channel_id=1, replica_groups=mesh['groups'=2,'tensor'=4,'section'=4] {'tensor'}, use_global_device_ids=true, to_apply=%region_2.2 | all-reduce | flops 8192 | bytes 65536 | tf_op jit(solution)/shard_map/while/body/eval_jaxpr/psum | solution.py:86
  706.1 10.9 %psum.25 = f32[16,512]{1,0:T(8,128)S(1)} all-reduce(f32[16,512]{1,0:T(8,128)S(1)} %fusion.54), channel_id=1, replica_groups=mesh['groups'=2,'tensor'=4,'section'=4] {'tensor'}, use_global_device_ids=true, to_apply=%region_2.2 | all-reduce | flops 8192 | bytes 65536 | tf_op jit(solution)/shard_map/while/body/eval_jaxpr/psum | solution.py:86
  752.1 11.4 %psum.25 = f32[16,512]{1,0:T(8,128)S(1)} all-reduce(f32[16,512]{1,0:T(8,128)S(1)} %fusion.54), channel_id=1, replica_groups=mesh['groups'=2,'tensor'=4,'section'=4] {'tensor'}, use_global_device_ids=true, to_apply=%region_2.2 | all-reduce | flops 8192 | bytes 65536 | tf_op jit(solution)/shard_map/while/body/eval_jaxpr/psum | solution.py:86
  798.5 10.9 %psum.25 = f32[16,512]{1,0:T(8,128)S(1)} all-reduce(f32[16,512]{1,0:T(8,128)S(1)} %fusion.54), channel_id=1, replica_groups=mesh['groups'=2,'tensor'=4,'section'=4] {'tensor'}, use_global_device_ids=true, to_apply=%region_2.2 | all-reduce | flops 8192 | bytes 65536 | tf_op jit(solution)/shard_map/while/body/eval_jaxpr/psum | solution.py:86
  844.5 11.4 %psum.25 = f32[16,512]{1,0:T(8,128)S(1)} all-reduce(f32[16,512]{1,0:T(8,128)S(1)} %fusion.54), channel_id=1, replica_groups=mesh['groups'=2,'tensor'=4,'section'=4] {'tensor'}, use_global_device_ids=true, to_apply=%region_2.2 | all-reduce | flops 8192 | bytes 65536 | tf_op jit(solution)/shard_map/while/body/eval_jaxpr/psum | solution.py:86
  890.9 10.9 %psum.25 = f32[16,512]{1,0:T(8,128)S(1)} all-reduce(f32[16,512]{1,0:T(8,128)S(1)} %fusion.54), channel_id=1, replica_groups=mesh['groups'=2,'tensor'=4,'section'=4] {'tensor'}, use_global_device_ids=true, to_apply=%region_2.2 | all-reduce | flops 8192 | bytes 65536 | tf_op jit(solution)/shard_map/while/body/eval_jaxpr/psum | solution.py:86
  936.9 11.4 %psum.25 = f32[16,512]{1,0:T(8,128)S(1)} all-reduce(f32[16,512]{1,0:T(8,128)S(1)} %fusion.54), channel_id=1, replica_groups=mesh['groups'=2,'tensor'=4,'section'=4] {'tensor'}, use_global_device_ids=true, to_apply=%region_2.2 | all-reduce | flops 8192 | bytes 65536 | tf_op jit(solution)/shard_map/while/body/eval_jaxpr/psum | solution.py:86
  958.0 36.9 %all-reduce.2.cloned.1.call-done = bf16[64,2048]{1,0:T(8,128)(2,1)} async-done(((bf16[64,2048]{1,0:T(8,128)(2,1)}), bf16[64,2048]{1,0:T(8,128)(2,1)}) %all-reduce.2.cloned.1.call-update) | async-done | bytes 262160 | tf_op jit(solution)/shard_map/psum | solution.py:17
  (169 shorter events, 278.7 us)
Async XLA Ops:
  13.4 48.0 %all-to-all-start.1 = ((bf16[4,128,3584]{1,0,2:T(4,128)(2,1)}), bf16[4,128,3584]{1,0,2:T(4,128)(2,1)}, u32[]{:S(2)}, u32[]{:S(2)}) async-start(bf16[4,128,3584]{1,0,2:T(4,128)(2,1)} %copy.26), calls=%async_computation.1 | async-start | bytes 7340032 | tf_op jit(solution)/shard_map/all_to_all | solution.py:39
  61.4 47.3 %all-to-all-start.4 = ((bf16[4,128,3584]{1,0,2:T(4,128)(2,1)}), bf16[4,128,3584]{1,0,2:T(4,128)(2,1)}, u32[]{:S(2)}, u32[]{:S(2)}) async-start(bf16[4,128,3584]{1,0,2:T(4,128)(2,1)} %copy.30), calls=%async_computation.4 | async-start | bytes 7340032 | tf_op jit(solution)/shard_map/all_to_all | solution.py:46
  73.0 83.8 %copy-start.6 = (bf16[4,128,2048]{2,1,0:T(8,128)(2,1)S(1)}, bf16[4,128,2048]{2,1,0:T(8,128)(2,1)}, u32[]{:S(2)}) copy-start(bf16[4,128,2048]{2,1,0:T(8,128)(2,1)} %param.14) | copy-start | bytes 6291460
  156.8 53.6 %copy-start.7 = (bf16[4,128,2048]{2,1,0:T(8,128)(2,1)S(1)}, bf16[4,128,2048]{2,1,0:T(8,128)(2,1)}, u32[]{:S(2)}) copy-start(bf16[4,128,2048]{2,1,0:T(8,128)(2,1)} %param.15) | copy-start | bytes 6291460
  260.8 50.9 %all-to-all-start.8 = ((bf16[4,2048,128]{2,1,0:T(8,128)(2,1)}), bf16[4,2048,128]{2,1,0:T(8,128)(2,1)S(1)}, u32[]{:S(2)}, u32[]{:S(2)}) async-start(bf16[4,2048,128]{2,1,0:T(8,128)(2,1)} %param.19), calls=%async_computation.8 | async-start | bytes 4194304 | tf_op jit(solution)/shard_map/all_to_all | solution.py:35
  311.7 1.3 copy-start.1
  313.0 86.3 %all-to-all-start.2 = ((bf16[4,512,896]{2,1,0:T(8,128)(2,1)}), bf16[4,512,896]{2,1,0:T(8,128)(2,1)}, u32[]{:S(2)}, u32[]{:S(2)}) async-start(bf16[4,512,896]{2,1,0:T(8,128)(2,1)} %bitcast.83), calls=%async_computation.2 | async-start | bytes 7340032 | tf_op jit(solution)/shard_map/all_to_all | solution.py:38
  399.3 86.3 %all-to-all-start.5 = ((bf16[4,512,896]{2,1,0:T(8,128)(2,1)}), bf16[4,512,896]{2,1,0:T(8,128)(2,1)}, u32[]{:S(2)}, u32[]{:S(2)}) async-start(bf16[4,512,896]{2,1,0:T(8,128)(2,1)} %bitcast.82), calls=%async_computation.5 | async-start | bytes 7340032 | tf_op jit(solution)/shard_map/all_to_all | solution.py:45
  485.6 5.0 copy-start.8
  485.6 94.0 %copy-start.9 = (s32[1,3]{1,0:T(1,128)S(1)}, s32[1,3]{1,0:T(1,128)}, u32[]{:S(2)}) copy-start(s32[1,3]{1,0:T(1,128)} %param.13) | copy-start | bytes 40
  485.6 94.6 %copy-start.4 = (bf16[4,128,2048]{2,1,0:T(8,128)(2,1)S(1)}, bf16[4,128,2048]{2,1,0:T(8,128)(2,1)}, u32[]{:S(2)}) copy-start(bf16[4,128,2048]{2,1,0:T(8,128)(2,1)} %all_to_all.145) | copy-start | bytes 6291460
  485.6 137.3 %all-to-all-start.7 = ((bf16[4,512,896]{2,1,0:T(8,128)(2,1)}), bf16[4,512,896]{2,1,0:T(8,128)(2,1)}, u32[]{:S(2)}, u32[]{:S(2)}) async-start(bf16[4,512,896]{2,1,0:T(8,128)(2,1)} %bitcast.80), calls=%async_computation.7 | async-start | bytes 7340032 | tf_op jit(solution)/shard_map/all_to_all | solution.py:52
  490.5 504.4 %all-reduce.2.cloned.1.call-start = ((), (), s32[]{:S(2)}) async-start(), calls=%async_computation.9 | async-start | bytes 524288 | tf_op jit(solution)/shard_map/psum | solution.py:17
  580.2 3.1 copy-start.3
  583.3 4.4 copy-start.2
  628.9 6.0 copy-start.5
  641.0 14.8 %copy-start = (bf16[512,3584]{1,0:T(8,128)(2,1)S(1)}, bf16[512,3584]{1,0:T(8,128)(2,1)}, u32[]{:S(2)}) copy-start(bf16[512,3584]{1,0:T(8,128)(2,1)} %get-tuple-element.710) | copy-start | bytes 11010052 | tf_op jit(solution)/shard_map/while
  675.3 4.8 collective-permute-start
  686.1 14.8 %copy-start = (bf16[512,3584]{1,0:T(8,128)(2,1)S(1)}, bf16[512,3584]{1,0:T(8,128)(2,1)}, u32[]{:S(2)}) copy-start(bf16[512,3584]{1,0:T(8,128)(2,1)} %get-tuple-element.710) | copy-start | bytes 11010052 | tf_op jit(solution)/shard_map/while
  719.8 6.2 collective-permute-start
  732.0 14.8 %copy-start = (bf16[512,3584]{1,0:T(8,128)(2,1)S(1)}, bf16[512,3584]{1,0:T(8,128)(2,1)}, u32[]{:S(2)}) copy-start(bf16[512,3584]{1,0:T(8,128)(2,1)} %get-tuple-element.710) | copy-start | bytes 11010052 | tf_op jit(solution)/shard_map/while
  766.3 6.2 collective-permute-start
  778.5 14.8 %copy-start = (bf16[512,3584]{1,0:T(8,128)(2,1)S(1)}, bf16[512,3584]{1,0:T(8,128)(2,1)}, u32[]{:S(2)}) copy-start(bf16[512,3584]{1,0:T(8,128)(2,1)} %get-tuple-element.710) | copy-start | bytes 11010052 | tf_op jit(solution)/shard_map/while
  812.2 6.2 collective-permute-start
  824.4 14.8 %copy-start = (bf16[512,3584]{1,0:T(8,128)(2,1)S(1)}, bf16[512,3584]{1,0:T(8,128)(2,1)}, u32[]{:S(2)}) copy-start(bf16[512,3584]{1,0:T(8,128)(2,1)} %get-tuple-element.710) | copy-start | bytes 11010052 | tf_op jit(solution)/shard_map/while
  858.7 6.2 collective-permute-start
  870.9 14.8 %copy-start = (bf16[512,3584]{1,0:T(8,128)(2,1)S(1)}, bf16[512,3584]{1,0:T(8,128)(2,1)}, u32[]{:S(2)}) copy-start(bf16[512,3584]{1,0:T(8,128)(2,1)} %get-tuple-element.710) | copy-start | bytes 11010052 | tf_op jit(solution)/shard_map/while
  904.6 6.2 collective-permute-start
  916.8 14.8 %copy-start = (bf16[512,3584]{1,0:T(8,128)(2,1)S(1)}, bf16[512,3584]{1,0:T(8,128)(2,1)}, u32[]{:S(2)}) copy-start(bf16[512,3584]{1,0:T(8,128)(2,1)} %get-tuple-element.710) | copy-start | bytes 11010052 | tf_op jit(solution)/shard_map/while
  951.1 6.2 collective-permute-start
Sparse Core Ops, SparseCore 0:
  958.1 36.7 all-reduce.1
where the time goes:
time: 1010 us; the launch traced here: 1000 us
  blocking collectives  432 us (43%)
  waiting for transfers between devices  312 us (31%)
  local copies, waits for them, and re-layouts  99.4 us (10%)
  matrix products  73.3 us (7%)
  starting transfers between devices  56.1 us (6%)
  other arithmetic  16.3 us (2%)
  between operations  13.5 us (1%)
    all_gather x1, blocking collectives, body(): prompt_rows = lax.all_gather(prompt, 'section', axis=0, tiled=True)  89 us
    psum x7, blocking collectives, layer_step(): summed = lax.psum(contract_last(hidden, down_rows), 'tensor')  78.1 us
    all_to_all x1, waiting for transfers between devices, body(): lax.all_to_all(lax.all_to_all(gate_right, 'tensor', split_axis=2, concat_...  74.6 us
    all_to_all x1, waiting for transfers between devices, body(): lax.all_to_all(lax.all_to_all(up_right, 'tensor', split_axis=2, concat_ax...  74.6 us
    dot_general x28, matrix products, contract_last(): lax.dot_general(left_side, right_side, (((1,), (1,)), ((), ())), preferre...  69.2 us
    all_to_all x1, blocking collectives, body(): lax.all_to_all(gate_left, 'section', split_axis=0, concat_axis=2, tiled=T...  53.6 us
    all_to_all x1, blocking collectives, body(): lax.all_to_all(up_left, 'section', split_axis=0, concat_axis=2, tiled=True)  50.4 us
    all_to_all x1, blocking collectives, body(): lax.all_to_all(down_left, 'tensor', split_axis=2, concat_axis=1, tiled=True)  48.1 us
  transfers between devices with their start and end apart: 14, of which 13 were waited for; matrix products, arithmetic and copies ran while one was open for 8% of the time, Pallas kernels for 0%

commit v1 on v0

--- a/solution.py
+++ b/solution.py
@@ -83,7 +83,7 @@
         gate_values = jnp.dot(gate_low, gate_cols, preferred_element_type=jnp.float32)
         up_values = jnp.dot(up_low, up_cols, preferred_element_type=jnp.float32)
         hidden = (jax.nn.silu(gate_values) * up_values).astype(jnp.bfloat16)
-        summed = lax.psum(contract_last(hidden, down_rows), "tensor")
+        summed = jnp.sum(lax.all_gather(contract_last(hidden, down_rows), "tensor"), axis=0)
         down_low = (summed * down_mask).astype(jnp.bfloat16)
         branch = contract_last(down_low, down_cols)
         own_columns = lax.dynamic_slice_in_dim(float_stream, own_start, column_block, 1)

time: 1010 us -> 967 us (0.957)
  blocking collectives: 432 us -> 392 us
    psum x7 -> x0, blocking collectives: 78.1 us -> none  [layer_step(): summed = lax.psum(contract_last(hidden, down_rows), 'tensor')]
    all_gather x0 -> x7, blocking collectives: none -> 38 us  [layer_step(): lax.all_gather(contract_last(hidden, down_rows), 'tensor')]
where the time goes in v1:
time: 967 us; the launch traced here: 964 us
  blocking collectives  392 us (41%)
  waiting for transfers between devices  312 us (32%)
  local copies, waits for them, and re-layouts  99.4 us (10%)
  matrix products  73.3 us (8%)
  starting transfers between devices  56.6 us (6%)
  other arithmetic  16.4 us (2%)
  between operations  13.5 us (1%)
    all_gather x1, blocking collectives, body(): prompt_rows = lax.all_gather(prompt, 'section', axis=0, tiled=True)  89 us
    all_to_all x1, waiting for transfers between devices, body(): lax.all_to_all(lax.all_to_all(gate_right, 'tensor', split_axis=2, concat_...  74.6 us
    all_to_all x1, waiting for transfers between devices, body(): lax.all_to_all(lax.all_to_all(up_right, 'tensor', split_axis=2, concat_ax...  74.6 us
    dot_general x28, matrix products, contract_last(): lax.dot_general(left_side, right_side, (((1,), (1,)), ((), ())), preferre...  69.2 us
    all_to_all x1, blocking collectives, body(): lax.all_to_all(gate_left, 'section', split_axis=0, concat_axis=2, tiled=T...  53.6 us
    all_to_all x1, blocking collectives, body(): lax.all_to_all(up_left, 'section', split_axis=0, concat_axis=2, tiled=True)  50.4 us
    all_to_all x1, blocking collectives, body(): lax.all_to_all(down_left, 'tensor', split_axis=2, concat_axis=1, tiled=True)  48.1 us
    unnamed x27, local copies, waits for them, and re-layouts  45.7 us
  transfers between devices with their start and end apart: 14, of which 13 were waited for; matrix products, arithmetic and copies ran while one was open for 8% of the time, Pallas kernels for 0%

profile of v1, /device:TPU:0, one launch (start us, length us, event | category | flops | bytes accessed | tf_op | source)
XLA Modules:
  0.0 964.2 jit_solution(6980734389071341305)
XLA Ops:
  6.5 6.8 copy.26
  18.2 6.9 copy.30
  25.0 36.4 %all-to-all-done.1 = bf16[4,128,3584]{1,0,2:T(4,128)(2,1)} async-done(((bf16[4,128,3584]{1,0,2:T(4,128)(2,1)}), bf16[4,128,3584]{1,0,2:T(4,128)(2,1)}, u32[]{:S(2)}, u32[]{:S(2)}) %all-to-all-start.1) | async-done | bytes 3670048 | tf_op jit(solution)/shard_map/all_to_all | solution.py:39
  66.2 6.9 copy.33
  73.0 35.7 %all-to-all-done.4 = bf16[4,128,3584]{1,0,2:T(4,128)(2,1)} async-done(((bf16[4,128,3584]{1,0,2:T(4,128)(2,1)}), bf16[4,128,3584]{1,0,2:T(4,128)(2,1)}, u32[]{:S(2)}, u32[]{:S(2)}) %all-to-all-start.4) | async-done | bytes 3670048 | tf_op jit(solution)/shard_map/all_to_all | solution.py:46
  108.7 48.1 %all_to_all.144 = bf16[4,128,3584]{1,0,2:T(4,128)(2,1)} all-to-all(bf16[4,128,3584]{1,0,2:T(4,128)(2,1)} %copy.33), channel_id=1, replica_groups=mesh['groups'=2,'tensor'=4,'section'=4] {'tensor'}, dimensions={2} | all-to-all | bytes 7340032 | tf_op jit(solution)/shard_map/all_to_all | solution.py:53
  156.8 53.6 %all_to_all.145 = bf16[4,128,2048]{2,1,0:T(8,128)(2,1)} all-to-all(bf16[4,128,2048]{2,1,0:T(8,128)(2,1)S(1)} %copy-done.6), channel_id=1, replica_groups=mesh['groups'=2,'tensor'=4,'section'=4] {'section'}, dimensions={0} | all-to-all | bytes 4194304 | tf_op jit(solution)/shard_map/all_to_all | solution.py:33
  210.4 50.4 %all_to_all.146 = bf16[4,128,2048]{2,1,0:T(8,128)(2,1)} all-to-all(bf16[4,128,2048]{2,1,0:T(8,128)(2,1)S(1)} %copy-done.7), channel_id=1, replica_groups=mesh['groups'=2,'tensor'=4,'section'=4] {'section'}, dimensions={0} | all-to-all | bytes 4194304 | tf_op jit(solution)/shard_map/all_to_all | solution.py:34
  264.5 6.9 copy.27
  271.3 40.4 %all-to-all-done.8 = bf16[4,2048,128]{2,1,0:T(8,128)(2,1)S(1)} async-done(((bf16[4,2048,128]{2,1,0:T(8,128)(2,1)}), bf16[4,2048,128]{2,1,0:T(8,128)(2,1)S(1)}, u32[]{:S(2)}, u32[]{:S(2)}) %all-to-all-start.8) | async-done | bytes 2097184 | tf_op jit(solution)/shard_map/all_to_all | solution.py:35
  317.8 6.9 copy.31
  324.7 74.6 %all-to-all-done.2 = bf16[4,512,896]{2,1,0:T(8,128)(2,1)} async-done(((bf16[4,512,896]{2,1,0:T(8,128)(2,1)}), bf16[4,512,896]{2,1,0:T(8,128)(2,1)}, u32[]{:S(2)}, u32[]{:S(2)}) %all-to-all-start.2) | async-done | bytes 3670048 | tf_op jit(solution)/shard_map/all_to_all | solution.py:38
  404.1 7.0 copy.34
  411.0 74.6 %all-to-all-done.5 = bf16[4,512,896]{2,1,0:T(8,128)(2,1)} async-done(((bf16[4,512,896]{2,1,0:T(8,128)(2,1)}), bf16[4,512,896]{2,1,0:T(8,128)(2,1)}, u32[]{:S(2)}, u32[]{:S(2)}) %all-to-all-start.5) | async-done | bytes 3670048 | tf_op jit(solution)/shard_map/all_to_all | solution.py:45
  490.6 89.0 %all_gather.53 = bf16[64,2048]{1,0:T(8,128)(2,1)S(1)} all-gather(bf16[16,2048]{1,0:T(8,128)(2,1)S(1)} %copy-done.8), channel_id=1, replica_groups=mesh['groups'=2,'tensor'=4,'section'=4] {'section'}, dimensions={0}, use_global_device_ids=true | all-gather | bytes 327680 | tf_op jit(solution)/shard_map/all_gather | solution.py:71
  587.6 9.7 %copy.36 = bf16[1,2048,4,128]{3,2,1,0:T(4,128)(2,1)S(1)} copy(bf16[1,2048,4,128]{3,1,2,0:T(8,128)(2,1)S(1)} %bitcast.91) | data formatting | bytes 4194304 | tf_op jit(solution)/shard_map/all_to_all | solution.py:35
  599.1 6.0 copy.28
  605.0 5.9 copy.37
  611.0 6.0 copy.32
  616.9 6.0 copy.38
  622.9 6.0 copy.35
  628.9 6.0 copy.39
  634.9 282.7 %while.19 = (s32[]{:T(128)}, bf16[16,2048]{1,0:T(8,128)(2,1)S(1)}, bf16[64,2048]{1,0:T(8,128)(2,1)S(1)}, pred[]{:T(512)}, bf16[64,2048]{1,0:T(8,128)(2,1)S(1)}, ...) while((s32[]{:T(128)}, bf16[16,2048]{1,0:T(8,128)(2,1)S(1)}, ...), condition=%wide.region_3.4_spmd.clone.clone, body=%wide.region_0.3_spmd.clone.clone.sunk | while | flops 278923040 | bytes 35674916 | solution.py:110
  635.0 5.8 all_gather.63
  661.0 5.4 all-gather.4
  674.1 5.8 all_gather.63
  714.7 5.8 all_gather.63
  755.3 5.8 all_gather.63
  795.9 5.8 all_gather.63
  836.5 5.8 all_gather.63
  877.1 5.8 all_gather.63
  918.4 37.5 %all-reduce.2.cloned.1.call-done = bf16[64,2048]{1,0:T(8,128)(2,1)} async-done(((bf16[64,2048]{1,0:T(8,128)(2,1)}), bf16[64,2048]{1,0:T(8,128)(2,1)}) %all-reduce.2.cloned.1.call-update) | async-done | bytes 262160 | tf_op jit(solution)/shard_map/psum | solution.py:17
  (176 shorter events, 277.1 us)
Async XLA Ops:
  13.4 48.0 %all-to-all-start.1 = ((bf16[4,128,3584]{1,0,2:T(4,128)(2,1)}), bf16[4,128,3584]{1,0,2:T(4,128)(2,1)}, u32[]{:S(2)}, u32[]{:S(2)}) async-start(bf16[4,128,3584]{1,0,2:T(4,128)(2,1)} %copy.26), calls=%async_computation.1 | async-start | bytes 7340032 | tf_op jit(solution)/shard_map/all_to_all | solution.py:39
  61.4 47.3 %all-to-all-start.4 = ((bf16[4,128,3584]{1,0,2:T(4,128)(2,1)}), bf16[4,128,3584]{1,0,2:T(4,128)(2,1)}, u32[]{:S(2)}, u32[]{:S(2)}) async-start(bf16[4,128,3584]{1,0,2:T(4,128)(2,1)} %copy.30), calls=%async_computation.4 | async-start | bytes 7340032 | tf_op jit(solution)/shard_map/all_to_all | solution.py:46
  73.0 83.8 %copy-start.6 = (bf16[4,128,2048]{2,1,0:T(8,128)(2,1)S(1)}, bf16[4,128,2048]{2,1,0:T(8,128)(2,1)}, u32[]{:S(2)}) copy-start(bf16[4,128,2048]{2,1,0:T(8,128)(2,1)} %param.14) | copy-start | bytes 6291460
  156.8 53.6 %copy-start.7 = (bf16[4,128,2048]{2,1,0:T(8,128)(2,1)S(1)}, bf16[4,128,2048]{2,1,0:T(8,128)(2,1)}, u32[]{:S(2)}) copy-start(bf16[4,128,2048]{2,1,0:T(8,128)(2,1)} %param.15) | copy-start | bytes 6291460
  260.8 50.9 %all-to-all-start.8 = ((bf16[4,2048,128]{2,1,0:T(8,128)(2,1)}), bf16[4,2048,128]{2,1,0:T(8,128)(2,1)S(1)}, u32[]{:S(2)}, u32[]{:S(2)}) async-start(bf16[4,2048,128]{2,1,0:T(8,128)(2,1)} %param.19), calls=%async_computation.8 | async-start | bytes 4194304 | tf_op jit(solution)/shard_map/all_to_all | solution.py:35
  311.7 1.3 copy-start.1
  313.0 86.3 %all-to-all-start.2 = ((bf16[4,512,896]{2,1,0:T(8,128)(2,1)}), bf16[4,512,896]{2,1,0:T(8,128)(2,1)}, u32[]{:S(2)}, u32[]{:S(2)}) async-start(bf16[4,512,896]{2,1,0:T(8,128)(2,1)} %bitcast.86), calls=%async_computation.2 | async-start | bytes 7340032 | tf_op jit(solution)/shard_map/all_to_all | solution.py:38
  399.3 86.3 %all-to-all-start.5 = ((bf16[4,512,896]{2,1,0:T(8,128)(2,1)}), bf16[4,512,896]{2,1,0:T(8,128)(2,1)}, u32[]{:S(2)}, u32[]{:S(2)}) async-start(bf16[4,512,896]{2,1,0:T(8,128)(2,1)} %bitcast.85), calls=%async_computation.5 | async-start | bytes 7340032 | tf_op jit(solution)/shard_map/all_to_all | solution.py:45
  485.6 5.0 copy-start.8
  485.6 94.0 %copy-start.9 = (s32[1,3]{1,0:T(1,128)S(1)}, s32[1,3]{1,0:T(1,128)}, u32[]{:S(2)}) copy-start(s32[1,3]{1,0:T(1,128)} %param.13) | copy-start | bytes 40
  485.6 94.6 %copy-start.4 = (bf16[4,128,2048]{2,1,0:T(8,128)(2,1)S(1)}, bf16[4,128,2048]{2,1,0:T(8,128)(2,1)}, u32[]{:S(2)}) copy-start(bf16[4,128,2048]{2,1,0:T(8,128)(2,1)} %all_to_all.145) | copy-start | bytes 6291460
  485.6 137.3 %all-to-all-start.7 = ((bf16[4,512,896]{2,1,0:T(8,128)(2,1)}), bf16[4,512,896]{2,1,0:T(8,128)(2,1)}, u32[]{:S(2)}, u32[]{:S(2)}) async-start(bf16[4,512,896]{2,1,0:T(8,128)(2,1)} %bitcast.83), calls=%async_computation.7 | async-start | bytes 7340032 | tf_op jit(solution)/shard_map/all_to_all | solution.py:52
  490.5 465.4 %all-reduce.2.cloned.1.call-start = ((), (), s32[]{:S(2)}) async-start(), calls=%async_computation.9 | async-start | bytes 524288 | tf_op jit(solution)/shard_map/psum | solution.py:17
  580.2 3.1 copy-start.3
  583.3 4.4 copy-start.2
  628.9 6.0 copy-start.5
  641.0 14.8 %copy-start = (bf16[512,3584]{1,0:T(8,128)(2,1)S(1)}, bf16[512,3584]{1,0:T(8,128)(2,1)}, u32[]{:S(2)}) copy-start(bf16[512,3584]{1,0:T(8,128)(2,1)} %get-tuple-element.712) | copy-start | bytes 11010052 | tf_op jit(solution)/shard_map/while
  669.3 4.8 collective-permute-start
  680.1 14.8 %copy-start = (bf16[512,3584]{1,0:T(8,128)(2,1)S(1)}, bf16[512,3584]{1,0:T(8,128)(2,1)}, u32[]{:S(2)}) copy-start(bf16[512,3584]{1,0:T(8,128)(2,1)} %get-tuple-element.712) | copy-start | bytes 11010052 | tf_op jit(solution)/shard_map/while
  708.5 6.2 collective-permute-start
  720.7 14.8 %copy-start = (bf16[512,3584]{1,0:T(8,128)(2,1)S(1)}, bf16[512,3584]{1,0:T(8,128)(2,1)}, u32[]{:S(2)}) copy-start(bf16[512,3584]{1,0:T(8,128)(2,1)} %get-tuple-element.712) | copy-start | bytes 11010052 | tf_op jit(solution)/shard_map/while
  749.0 6.2 collective-permute-start
  761.3 14.8 %copy-start = (bf16[512,3584]{1,0:T(8,128)(2,1)S(1)}, bf16[512,3584]{1,0:T(8,128)(2,1)}, u32[]{:S(2)}) copy-start(bf16[512,3584]{1,0:T(8,128)(2,1)} %get-tuple-element.712) | copy-start | bytes 11010052 | tf_op jit(solution)/shard_map/while
  789.6 6.2 collective-permute-start
  801.9 14.8 %copy-start = (bf16[512,3584]{1,0:T(8,128)(2,1)S(1)}, bf16[512,3584]{1,0:T(8,128)(2,1)}, u32[]{:S(2)}) copy-start(bf16[512,3584]{1,0:T(8,128)(2,1)} %get-tuple-element.712) | copy-start | bytes 11010052 | tf_op jit(solution)/shard_map/while
  830.2 6.2 collective-permute-start
  842.5 14.8 %copy-start = (bf16[512,3584]{1,0:T(8,128)(2,1)S(1)}, bf16[512,3584]{1,0:T(8,128)(2,1)}, u32[]{:S(2)}) copy-start(bf16[512,3584]{1,0:T(8,128)(2,1)} %get-tuple-element.712) | copy-start | bytes 11010052 | tf_op jit(solution)/shard_map/while
  870.8 6.2 collective-permute-start
  883.1 14.8 %copy-start = (bf16[512,3584]{1,0:T(8,128)(2,1)S(1)}, bf16[512,3584]{1,0:T(8,128)(2,1)}, u32[]{:S(2)}) copy-start(bf16[512,3584]{1,0:T(8,128)(2,1)} %get-tuple-element.712) | copy-start | bytes 11010052 | tf_op jit(solution)/shard_map/while
  911.4 6.2 collective-permute-start
Sparse Core Ops, SparseCore 0:
  918.5 37.3 all-reduce.1
